TPU v7x, 32 devices: a whole 2x2x4 slice. The times are simulated.
32 devices in a mesh: groups: 2 (over y), ctx: 8 (over z, x), kvh: 2 (over core).
Axes of the slice: x: 2, y: 2, z: 4, core: 2. Of those that a mesh axis runs over, the one named last changes fastest.
Arguments:
- queries: bfloat16 [2048, 4, 8, 128], P(('groups', 'ctx'), 'kvh'), parts along dimension 0, may hold values from -120 to 120
- keys: bfloat16 [2048, 4, 128], P(('groups', 'ctx'), 'kvh'), parts along dimension 0, may hold values from -8 to 8
- values: bfloat16 [2048, 4, 128], P(('groups', 'ctx'), 'kvh'), parts along dimension 0, may hold values from -6 to 6
- seq_lengths: int32 [8], P('groups'), parts along dimension 0, may hold values from 1 to 768, 1024 in all
Outputs:
- attended: bfloat16 [2048, 4, 8, 128], P(('groups', 'ctx'), 'kvh'), parts along dimension 0
There are 2 independent parts, one for each index of `groups`. A program takes and returns all parts, laid end to end along the dimension named above; each array names one. Nothing has to cross between parts.
Inputs may be any that keep to these rules, and one draw needn't show every extreme that they name: `seq_lengths`: sum to 1024; the longest is exactly 768.
All inputs are finite; a program needn't handle non-finite values.
Results may differ from a plain program's by a relative error of at most 0.005.
Values may be sent and summed in bfloat16 or wider, within the bound.
No kernel may reach another device: no remote copies, remote signals or barrier semaphores. Data moves between devices by JAX's collectives and lax.ppermute only.
A program may use at most 64 MiB of HBM per device.

v0:
```python
import math
import jax
import jax.numpy as jnp
from jax import lax
from jax.sharding import PartitionSpec as P


def seq_index(positions, starts):
    return jnp.sum((positions[:, None] >= starts[None, :]).astype(jnp.int32), axis=1)


def attend(work_queries, work_pos, keys, values, starts):
    row_count, local_heads, group_size, head_size = work_queries.shape
    score_scale = 1.0 / math.sqrt(head_size)
    query_seq = seq_index(work_pos, starts)
    last_pos = jnp.max(work_pos)
    first_needed = jnp.min(starts[query_seq - 1])
    initial = (
        jnp.full((row_count, local_heads, group_size), -1e30, jnp.float32),
        jnp.zeros((row_count, local_heads, group_size), jnp.float32),
        jnp.zeros((row_count, local_heads, group_size, head_size), jnp.float32),
    )
    first_row = jnp.int32(0)
    key_piece = lax.all_gather(keys, "ctx", axis=0, tiled=True)
    value_piece = lax.all_gather(values, "ctx", axis=0, tiled=True)
    piece_rows = key_piece.shape[0]
    tile_rows = math.gcd(piece_rows, 512)
    tile_count = piece_rows // tile_rows

    def one_tile(running, inputs):
        key_tile, value_tile, offset = inputs
        key_pos = offset + jnp.arange(tile_rows, dtype=jnp.int32)
        key_seq = seq_index(key_pos, starts)
        allowed = (key_seq[None, :] == query_seq[:, None]) & (key_pos[None, :] <= work_pos[:, None])
        scores = (
            jnp.einsum("rkgd,tkd->rkgt", work_queries, key_tile, preferred_element_type=jnp.float32)
            * score_scale
        )
        scores = jnp.where(allowed[:, None, None, :], scores, -jnp.inf)
        running_max, running_sum, weighted = running
        new_max = jnp.maximum(running_max, jnp.max(scores, axis=3))
        factor = jnp.exp(running_max - new_max)
        weights = jnp.exp(scores - new_max[..., None])
        new_sum = running_sum * factor + jnp.sum(weights, axis=3)
        product = jnp.einsum(
            "rkgt,tkd->rkgd",
            weights.astype(jnp.bfloat16),
            value_tile,
            preferred_element_type=jnp.float32,
        )
        return ((new_max, new_sum, weighted * factor[..., None] + product), None)

    key_tiles = key_piece.reshape(tile_count, tile_rows, local_heads, head_size)
    value_tiles = value_piece.reshape(tile_count, tile_rows, local_heads, head_size)
    offsets = jnp.arange(tile_count, dtype=jnp.int32) * tile_rows

    def run_tiles(running):
        return lax.scan(one_tile, running, (key_tiles, value_tiles, offsets))[0]

    visible = (first_row <= last_pos) & (first_row + piece_rows - 1 >= first_needed)
    running_max, running_sum, weighted = lax.cond(
        visible, run_tiles, lambda running: running, initial
    )
    return (weighted / running_sum[..., None]).astype(jnp.bfloat16)


def on_device(queries, keys, values, seq_lengths):
    row_count = queries.shape[0]
    my_index = lax.axis_index("ctx")
    starts = jnp.cumsum(seq_lengths) - seq_lengths
    own_pos = my_index * row_count + jnp.arange(row_count, dtype=jnp.int32)
    return attend(queries, own_pos, keys, values, starts)


def solution(mesh):
    placed = (
        P(("groups", "ctx"), "kvh", None, None),
        P(("groups", "ctx"), "kvh", None),
        P(("groups", "ctx"), "kvh", None),
        P("groups"),
    )
    return jax.shard_map(
        on_device,
        mesh=mesh,
        in_specs=placed,
        out_specs=P(("groups", "ctx"), "kvh", None, None),
        check_vma=False,
    )
```

profile of v0, /device:TPU:0, one launch (start us, length us, event | category | flops | bytes accessed | tf_op | source)
XLA Modules:
  0.0 96.8 jit_solution(3941921183998855034)
XLA Ops:
  0.0 0.8 reduce-window.9
  0.8 0.7 bitcast_subtract_fusion
  1.5 0.1 convert_reduce_fusion.1
  1.6 0.6 fusion.27
  2.2 3.2 %fusion.25 = s32[]{:T(128)} fusion(s32[128]{0:T(128)S(1)} %convert_reduce_fusion.1, s32[]{:T(128)} %bitcast.6, s32[]{:T(128)} %bitcast.7, s32[]{:T(128)} %bitcast.9, s32[]{:T(128)} %bitcast.8), kind=kLoop, calls=%fused_computation.36 | loop fusion | flops 1407 | bytes 532 | tf_op jit(solution)/shard_map/reduce_min | solution.py:17
  6.1 0.6 fusion.26
  7.3 0.9 copy.21
  8.2 33.0 %all_gather.6 = bf16[1024,2,128]{2,0,1:T(8,128)(2,1)S(1)} all-gather(bf16[128,2,128]{2,0,1:T(8,128)(2,1)S(1)} %copy.21), channel_id=1, replica_groups=mesh['groups'=2,'ctx'=8,'kvh'=2] {'ctx'}, dimensions={0}, use_global_device_ids=true | all-gather | bytes 589824 | tf_op jit(solution)/shard_map/all_gather | solution.py:24
  41.2 0.8 copy.22
  42.1 31.3 %all_gather.7 = bf16[1024,2,128]{2,0,1:T(8,128)(2,1)S(1)} all-gather(bf16[128,2,128]{2,0,1:T(8,128)(2,1)S(1)} %copy.22), channel_id=1, replica_groups=mesh['groups'=2,'ctx'=8,'kvh'=2] {'ctx'}, dimensions={0}, use_global_device_ids=true | all-gather | bytes 589824 | tf_op jit(solution)/shard_map/all_gather | solution.py:25
  73.4 21.4 %conditional.1 = (f32[128,2,8]{0,2,1:T(8,128)}, f32[128,2,8,128]{3,2,1,0:T(8,128)S(1)}) conditional(s32[]{:T(128)} %convert_element_type.16, () %tuple.20, (bf16[1024,2,128]{2,0,1:T(8,128)(2,1)S(1)}, bf16[1024,2,128]{2,0,1:T(8,128)(2,1)S(1)}, s32[2]{0:T(128)S(1)}, s32[4]{0:T(128)S(1)}, s32[128]{0:T(128)S(1)}, /*index=5*/s32[128]{0:T(128)S(1)}, ...), branch_computations={%region_4.5_spmd, %region_5.11_spmd} | conditional | flops 549404672 | bytes 36056412 | solution.py:61
  73.4 1.2 %copy.23 = bf16[128,2,8,128]{3,0,2,1:T(8,128)(2,1)S(1)} copy(bf16[128,2,8,128]{3,2,1,0:T(8,128)(2,1)} %get-tuple-element.187) | data formatting | bytes 1048576 | tf_op jit(solution)/shard_map
  74.6 19.7 %while.18 = (s32[]{:T(128)}, f32[128,2,8]{0,2,1:T(8,128)S(1)}, f32[128,2,8]{0,2,1:T(8,128)}, f32[128,2,8,128]{0,3,2,1:T(8,128)S(1)}, s32[2]{0:T(128)S(1)}, /*ind...) while((s32[]{:T(128)}, f32[128,2,8]{0,2,1:T(8,128)S(1)}, ...), condition=%wide.region_10.10_spmd.clone, body=%wide.region_6.9_spmd.clone.sunk | while | flops 549404672 | bytes 32910540 | solution.py:58
  74.6 0.7 dynamic_slice.29
  75.3 0.7 iota_add_fusion.3
  76.0 0.1 convert_reduce_fusion.3
  76.0 0.2 compare_and_fusion.2
  76.3 2.6 %fusion.39 = (f32[128,2,8]{0,2,1:T(8,128)S(1)}, f32[2,512,128,8]{2,1,3,0:T(8,128)}) fusion(pred[128,512]{0,1:T(8,128)(4,1)S(1)} %compare_and_fusion.2, bf16[128,2,8,128]{3,0,2,1:T(8,128)(2,1)S(1)} %get-tuple-element.329, bf16[2,512,2,128]{3,1,0,2:T(8,128)(2,1)S(1)} %get-tuple-element.328, s32[]{:T(128)} %get-tuple-element.307), kind=kOutput, calls=%fused_computation.4.clone.1 | convolution fusion | flops 271579136 | bytes 5054468 | tf_op jit(solution)/shard_map/cond/branch_1_fun/while/body/eval_jaxpr/rkgd,tkd->rkgt/dot_general | solution.py:36
  78.9 0.0 copy-start
  78.9 3.2 %fusion.40 = f32[128,2,8]{0,2,1:T(8,128)S(1)} fusion(f32[2,512,128,8]{2,1,3,0:T(8,128)} %get-tuple-element.291, f32[128,2,8]{0,2,1:T(8,128)S(1)} %select_maximum_fusion.2, pred[128,512]{0,1:T(8,128)(4,1)S(1)} %compare_and_fusion.2), kind=kLoop, calls=%fused_computation.3.clone.1 | loop fusion | flops 4192256 | bytes 4276224 | tf_op jit(solution)/shard_map/cond/branch_1_fun/while/body/eval_jaxpr/reduce_sum | solution.py:44
  82.1 0.6 fusion.41
  82.7 0.0 copy-done
  82.7 1.3 %fusion.42 = f32[128,2,8,128]{0,3,2,1:T(8,128)S(1)} fusion(f32[2,512,128,8]{2,1,3,0:T(8,128)S(1)} %copy-done, f32[128,2,8]{0,2,1:T(8,128)S(1)} %select_maximum_fusion.2, pred[128,512]{0,1:T(8,128)(4,1)S(1)} %compare_and_fusion.2, f32[128,2,8,128]{0,3,2,1:T(8,128)S(1)} %get-tuple-element.310, f32[128,2,8]{0,2,1:T(8,128)S(1)} %get-tuple-element.293, ...), kind=kOutput, calls=%fused_computation.11.clone.1 | convolution fusion | flops 273416192 | bytes 6635525 | tf_op jit(solution)/shard_map/cond/branch_1_fun/while/body/eval_jaxpr/rkgt,tkd->rkgd/dot_general | solution.py:45
  84.1 0.7 dynamic_slice.29
  84.8 0.7 iota_add_fusion.3
  85.5 0.1 convert_reduce_fusion.3
  85.5 0.2 compare_and_fusion.2
  85.8 2.6 %fusion.39 = (f32[128,2,8]{0,2,1:T(8,128)S(1)}, f32[2,512,128,8]{2,1,3,0:T(8,128)}) fusion(pred[128,512]{0,1:T(8,128)(4,1)S(1)} %compare_and_fusion.2, bf16[128,2,8,128]{3,0,2,1:T(8,128)(2,1)S(1)} %get-tuple-element.329, bf16[2,512,2,128]{3,1,0,2:T(8,128)(2,1)S(1)} %get-tuple-element.328, s32[]{:T(128)} %get-tuple-element.307), kind=kOutput, calls=%fused_computation.4.clone.1 | convolution fusion | flops 271579136 | bytes 5054468 | tf_op jit(solution)/shard_map/cond/branch_1_fun/while/body/eval_jaxpr/rkgd,tkd->rkgt/dot_general | solution.py:36
  88.4 0.0 copy-start
  88.4 3.2 %fusion.40 = f32[128,2,8]{0,2,1:T(8,128)S(1)} fusion(f32[2,512,128,8]{2,1,3,0:T(8,128)} %get-tuple-element.291, f32[128,2,8]{0,2,1:T(8,128)S(1)} %select_maximum_fusion.2, pred[128,512]{0,1:T(8,128)(4,1)S(1)} %compare_and_fusion.2), kind=kLoop, calls=%fused_computation.3.clone.1 | loop fusion | flops 4192256 | bytes 4276224 | tf_op jit(solution)/shard_map/cond/branch_1_fun/while/body/eval_jaxpr/reduce_sum | solution.py:44
  91.6 1.3 %fusion.41 = (f32[128,2,8]{0,2,1:T(8,128)}, f32[128,2,8]{0,2,1:T(8,128)S(1)}) fusion(f32[128,2,8]{0,2,1:T(8,128)S(1)} %fusion.40, f32[128,2,8]{0,2,1:T(8,128)} %get-tuple-element.309, pred[]{:T(512)S(6)} %compare.26, f32[128,2,8]{0,2,1:T(8,128)S(1)} %select_maximum_fusion.2, f32[128,2,8]{0,2,1:T(8,128)S(1)} %get-tuple-element.308), kind=kLoop, calls=%fused_computation.20.clone.1 | loop fusion | flops 10240 | bytes 49153 | tf_op jit(solution)/shard_map/cond/branch_1_fun/while/body/eval_jaxpr/add | solution.py:44
  92.9 0.0 copy-done
  92.9 1.3 %fusion.42 = f32[128,2,8,128]{0,3,2,1:T(8,128)S(1)} fusion(f32[2,512,128,8]{2,1,3,0:T(8,128)S(1)} %copy-done, f32[128,2,8]{0,2,1:T(8,128)S(1)} %select_maximum_fusion.2, pred[128,512]{0,1:T(8,128)(4,1)S(1)} %compare_and_fusion.2, f32[128,2,8,128]{0,3,2,1:T(8,128)S(1)} %get-tuple-element.310, f32[128,2,8]{0,2,1:T(8,128)S(1)} %get-tuple-element.293, ...), kind=kOutput, calls=%fused_computation.11.clone.1 | convolution fusion | flops 273416192 | bytes 6635525 | tf_op jit(solution)/shard_map/cond/branch_1_fun/while/body/eval_jaxpr/rkgt,tkd->rkgd/dot_general | solution.py:45
  94.3 0.5 copy.30
  94.8 0.8 copy.24
  95.6 1.1 %divide_convert_fusion = bf16[128,2,8,128]{3,2,1,0:T(8,128)(2,1)} fusion(f32[128,2,8,128]{3,2,1,0:T(8,128)S(1)} %get-tuple-element.188, f32[128,2,8]{2,1,0:T(2,128)S(1)} %copy.24), kind=kLoop, calls=%fused_computation.30 | loop fusion | flops 524288 | bytes 1581056 | tf_op jit(solution)/shard_map/convert_element_type | solution.py:64
  (10 shorter events, 0.0 us)
Async XLA Ops:
  78.9 3.8 %copy-start = (f32[2,512,128,8]{2,1,3,0:T(8,128)S(1)}, f32[2,512,128,8]{2,1,3,0:T(8,128)}, u32[]{:S(2)}) copy-start(f32[2,512,128,8]{2,1,3,0:T(8,128)} %get-tuple-element.291) | copy-start | bytes 12582916 | tf_op jit(solution)/shard_map/cond/branch_1_fun/while
  88.4 4.5 %copy-start = (f32[2,512,128,8]{2,1,3,0:T(8,128)S(1)}, f32[2,512,128,8]{2,1,3,0:T(8,128)}, u32[]{:S(2)}) copy-start(f32[2,512,128,8]{2,1,3,0:T(8,128)} %get-tuple-element.291) | copy-start | bytes 12582916 | tf_op jit(solution)/shard_map/cond/branch_1_fun/while
where the time goes:
time: 97.2 us; the launch traced here: 96.8 us
  blocking collectives  64.3 us (66%)
  other arithmetic  16.9 us (17%)
  matrix products  7.91 us (8%)
  local copies, waits for them, and re-layouts  6.19 us (6%)
  between operations  1.32 us (1%)
    all_gather x1, blocking collectives, attend(): key_piece = lax.all_gather(keys, 'ctx', axis=0, tiled=True)  33 us
    all_gather x1, blocking collectives, attend(): value_piece = lax.all_gather(values, 'ctx', axis=0, tiled=True)  31.3 us
    reduce_sum x2, other arithmetic, one_tile(): new_sum = running_sum * factor + jnp.sum(weights, axis=3)  6.42 us
    dot_general x2, matrix products, one_tile(): jnp.einsum('rkgd,tkd->rkgt', work_queries, key_tile, preferred_element_ty...  5.28 us
    reduce_min x1, other arithmetic, attend(): first_needed = jnp.min(starts[query_seq - 1])  3.22 us
    dot_general x2, matrix products, one_tile(): jnp.einsum('rkgt,tkd->rkgd', weights.astype(jnp.bfloat16), value_tile, pr...  2.64 us

commit v1 on v0

--- a/solution.py
+++ b/solution.py
@@ -3,6 +3,20 @@
 import jax.numpy as jnp
 from jax import lax
 from jax.sharding import PartitionSpec as P
+
+
+def classes_draw(view):
+    device_axis = "ctx"
+    odd = jax.lax.axis_index(device_axis)
+    front = jax.lax.axis_size(device_axis)
+    b_next, extra, t_next = (front, odd, view.shape[0])
+    view_out, outcome_arr = (view, 1)
+    while outcome_arr < b_next:
+        tile_out = tuple(((h, (h - outcome_arr) % b_next) for h in range(b_next)))
+        block_out = jax.lax.ppermute(view_out, device_axis, tile_out)
+        view_out = jnp.concatenate([view_out, block_out], axis=0)
+        outcome_arr = 2 * outcome_arr
+    return jnp.roll(view_out, extra * t_next, 0)
 
 
 def seq_index(positions, starts):
@@ -21,7 +35,7 @@
         jnp.zeros((row_count, local_heads, group_size, head_size), jnp.float32),
     )
     first_row = jnp.int32(0)
-    key_piece = lax.all_gather(keys, "ctx", axis=0, tiled=True)
+    key_piece = classes_draw(keys)
     value_piece = lax.all_gather(values, "ctx", axis=0, tiled=True)
     piece_rows = key_piece.shape[0]
     tile_rows = math.gcd(piece_rows, 512)

time: 97.2 us -> 82.1 us (0.84)
  blocking collectives: 64.3 us -> 31.5 us
  waiting for transfers between devices: 0 us -> 8.97 us
  starting transfers between devices: 0 us -> 7.42 us
  local copies, waits for them, and re-layouts: 6.19 us -> 7.34 us
    all_gather x1 -> x0, blocking collectives: 33 us -> none  [attend(): key_piece = lax.all_gather(keys, 'ctx', axis=0, tiled=True)]
    ppermute x0 -> x3, waiting for transfers between devices: none -> 8.97 us  [classes_draw(): block_out = jax.lax.ppermute(view_out, device_axis, tile_out)]
    ppermute x0 -> x3, starting transfers between devices: none -> 7.42 us  [classes_draw(): block_out = jax.lax.ppermute(view_out, device_axis, tile_out)]
    unnamed x2 -> x8, local copies, waits for them, and re-layouts: 1.7 us -> 2.67 us
  transfers between devices with their start and end apart: 0 -> 3, of which waited for: 0 -> 2; matrix products, arithmetic and copies ran while one was open for 0% -> 8% of each run, Pallas kernels for 0% -> 0%
where the time goes in v1:
time: 82.1 us; the launch traced here: 81.7 us
  blocking collectives  31.5 us (38%)
  other arithmetic  16.9 us (21%)
  waiting for transfers between devices  8.97 us (11%)
  matrix products  7.91 us (10%)
  starting transfers between devices  7.42 us (9%)
  local copies, waits for them, and re-layouts  7.34 us (9%)
  between operations  1.37 us (2%)
    all_gather x1, blocking collectives, attend(): value_piece = lax.all_gather(values, 'ctx', axis=0, tiled=True)  31.5 us
    ppermute x3, waiting for transfers between devices, classes_draw(): block_out = jax.lax.ppermute(view_out, device_axis, tile_out)  8.97 us
    ppermute x3, starting transfers between devices, classes_draw(): block_out = jax.lax.ppermute(view_out, device_axis, tile_out)  7.42 us
    reduce_sum x2, other arithmetic, one_tile(): new_sum = running_sum * factor + jnp.sum(weights, axis=3)  6.42 us
    dot_general x2, matrix products, one_tile(): jnp.einsum('rkgd,tkd->rkgt', work_queries, key_tile, preferred_element_ty...  5.27 us
    reduce_min x1, other arithmetic, attend(): first_needed = jnp.min(starts[query_seq - 1])  3.22 us
    unnamed x8, local copies, waits for them, and re-layouts  2.67 us
    dot_general x2, matrix products, one_tile(): jnp.einsum('rkgt,tkd->rkgd', weights.astype(jnp.bfloat16), value_tile, pr...  2.64 us
  transfers between devices with their start and end apart: 3, of which 2 were waited for; matrix products, arithmetic and copies ran while one was open for 8% of the time, Pallas kernels for 0%

profile of v1, /device:TPU:0, one launch (start us, length us, event | category | flops | bytes accessed | tf_op | source)
XLA Modules:
  0.0 81.7 jit_solution(14678608644459794908)
XLA Ops:
  0.0 0.9 %fusion.26 = (bf16[128,2,128]{2,0,1:T(8,128)(2,1)S(1)}, bf16[2048,2,128]{2,0,1:T(8,128)(2,1)S(1)}) fusion(bf16[128,2,128]{2,1,0:T(2,128)(2,1)} %param.9), kind=kLoop, calls=%fused_computation.51 | loop fusion | bytes 196608 | tf_op args[1]
  0.9 6.0 %collective-permute-start = (bf16[128,2,128]{2,0,1:T(8,128)(2,1)S(1)}, bf16[128,2,128]{2,0,1:T(8,128)(2,1)S(1)}, u32[]{:S(2)}, u32[]{:S(2)}) collective-permute-start(bf16[128,2,128]{2,0,1:T(8,128)(2,1)S(1)} %get-tuple-element.329), channel_id=1, source_target_pairs={{0,14},{2,0},{4,2},{6,4},{8,6},{10,8},{12,10},{14,12},{1,15},{3,1}... | collective-permute-start | bytes 196616 | tf_op jit(solution)/shard_map/ppermute | solution.py:16
  6.9 0.8 %reduce-window.9 = s32[4,1]{0,1:T(1,128)S(1)} reduce-window(s32[4,1]{0,1:T(1,128)} %bitcast.67, s32[]{:T(128)} %constant.90.clone.1), window={size=4x1 pad=3_0x0_0}, to_apply=%region_1.2 | reduce-window | flops 12 | bytes 36 | tf_op jit(solution)/shard_map/reduce-window.4
  7.7 0.7 bitcast_subtract_fusion
  8.4 0.8 %copy.30 = bf16[128,2,128]{2,0,1:T(8,128)(2,1)S(1)} copy(bf16[128,2,128]{2,1,0:T(2,128)(2,1)} %param.10) | data formatting | bytes 131072 | tf_op args[2]
  9.2 31.5 %all_gather.3 = bf16[1024,2,128]{2,0,1:T(8,128)(2,1)S(1)} all-gather(bf16[128,2,128]{2,0,1:T(8,128)(2,1)S(1)} %copy.30), channel_id=1, replica_groups=mesh['groups'=2,'ctx'=8,'kvh'=2] {'ctx'}, dimensions={0}, use_global_device_ids=true | all-gather | bytes 589824 | tf_op jit(solution)/shard_map/all_gather | solution.py:39
  40.7 0.6 fusion.27
  41.4 0.0 collective-permute-done
  41.4 0.6 collective-permute-start.1
  42.0 0.1 convert_reduce_fusion.1
  42.1 4.8 %collective-permute-done.1 = bf16[256,2,128]{2,0,1:T(8,128)(2,1)S(1)} collective-permute-done((bf16[256,2,128]{2,0,1:T(8,128)(2,1)S(1)}, bf16[256,2,128]{2,0,1:T(8,128)(2,1)S(1)}, u32[]{:S(2)}, u32[]{:S(2)}) %collective-permute-start.1) | collective-permute-done | bytes 131104 | tf_op jit(solution)/shard_map/ppermute | solution.py:16
  46.9 0.8 collective-permute-start.2
  47.7 3.2 %fusion.25 = s32[]{:T(128)} fusion(s32[128]{0:T(128)S(1)} %convert_reduce_fusion.1, s32[]{:T(128)} %bitcast.6, s32[]{:T(128)} %bitcast.7, s32[]{:T(128)} %bitcast.9, s32[]{:T(128)} %bitcast.8), kind=kLoop, calls=%fused_computation.49 | loop fusion | flops 1407 | bytes 532 | tf_op jit(solution)/shard_map/reduce_min | solution.py:31
  50.9 0.6 add_reduce_fusion
  52.9 4.2 %collective-permute-done.2 = bf16[512,2,128]{2,0,1:T(8,128)(2,1)S(1)} collective-permute-done((bf16[512,2,128]{2,0,1:T(8,128)(2,1)S(1)}, bf16[512,2,128]{2,0,1:T(8,128)(2,1)S(1)}, u32[]{:S(2)}, u32[]{:S(2)}) %collective-permute-start.2) | collective-permute-done | bytes 262176 | tf_op jit(solution)/shard_map/ppermute | solution.py:16
  57.1 0.9 %constant_dynamic-update-slice_fusion.3 = bf16[2048,2,128]{2,0,1:T(8,128)(2,1)S(1)} fusion(bf16[2048,2,128]{2,0,1:T(8,128)(2,1)S(1)} %constant_dynamic-update-slice_fusion.4, bf16[128,2,128]{2,1,0:T(2,128)(2,1)} %param.9), kind=kLoop, calls=%fused_computation.37 | loop fusion | bytes 131072
  58.1 21.6 %conditional.1 = (f32[128,2,8]{0,2,1:T(8,128)}, f32[128,2,8,128]{3,2,1,0:T(8,128)S(1)}) conditional(s32[]{:T(128)} %convert_element_type.16, () %tuple.32, (s32[]{:T(128)}, s32[]{:T(128)}, bf16[2048,2,128]{2,0,1:T(8,128)(2,1)S(1)}, bf16[1024,2,128]{2,0,1:T(8,128)(2,1)S(1)}, s32[2]{0:T(128)S(1)}, /*index=5*/s32[4]{0:T(128)S(1)}, s32[128]{0:T(128)S(1)}, ...), branch_computations={%region_4.5_spmd, %region_5.11_spmd} | conditional | flops 549404672 | bytes 37105148 | solution.py:75
  58.1 0.1 constant_dynamic-slice_fusion
  58.3 1.2 %copy.31 = bf16[128,2,8,128]{3,0,2,1:T(8,128)(2,1)S(1)} copy(bf16[128,2,8,128]{3,2,1,0:T(8,128)(2,1)} %get-tuple-element.296) | data formatting | bytes 1048576 | tf_op jit(solution)/shard_map
  59.5 19.7 %while.26 = (s32[]{:T(128)}, f32[128,2,8]{0,2,1:T(8,128)S(1)}, f32[128,2,8]{0,2,1:T(8,128)}, f32[128,2,8,128]{0,3,2,1:T(8,128)S(1)}, s32[2]{0:T(128)S(1)}, /*ind...) while((s32[]{:T(128)}, f32[128,2,8]{0,2,1:T(8,128)S(1)}, ...), condition=%wide.region_10.10_spmd.clone, body=%wide.region_6.9_spmd.clone.sunk | while | flops 549404672 | bytes 32910540 | solution.py:72
  59.5 0.7 dynamic_slice.40
  60.1 0.7 iota_add_fusion.3
  60.8 0.1 convert_reduce_fusion.3
  60.9 0.2 compare_and_fusion.2
  61.1 2.6 %fusion.39 = (f32[128,2,8]{0,2,1:T(8,128)S(1)}, f32[2,512,128,8]{2,1,3,0:T(8,128)}) fusion(pred[128,512]{0,1:T(8,128)(4,1)S(1)} %compare_and_fusion.2, bf16[128,2,8,128]{3,0,2,1:T(8,128)(2,1)S(1)} %get-tuple-element.445, bf16[2,512,2,128]{3,1,0,2:T(8,128)(2,1)S(1)} %get-tuple-element.444, s32[]{:T(128)} %get-tuple-element.423), kind=kOutput, calls=%fused_computation.4.clone.1 | convolution fusion | flops 271579136 | bytes 5054468 | tf_op jit(solution)/shard_map/cond/branch_1_fun/while/body/eval_jaxpr/rkgd,tkd->rkgt/dot_general | solution.py:50
  63.8 0.0 copy-start
  63.8 3.2 %fusion.40 = f32[128,2,8]{0,2,1:T(8,128)S(1)} fusion(f32[2,512,128,8]{2,1,3,0:T(8,128)} %get-tuple-element.407, f32[128,2,8]{0,2,1:T(8,128)S(1)} %select_maximum_fusion.2, pred[128,512]{0,1:T(8,128)(4,1)S(1)} %compare_and_fusion.2), kind=kLoop, calls=%fused_computation.3.clone.1 | loop fusion | flops 4192256 | bytes 4276224 | tf_op jit(solution)/shard_map/cond/branch_1_fun/while/body/eval_jaxpr/reduce_sum | solution.py:58
  67.0 0.6 fusion.41
  67.6 0.0 copy-done
  67.6 1.3 %fusion.42 = f32[128,2,8,128]{0,3,2,1:T(8,128)S(1)} fusion(f32[2,512,128,8]{2,1,3,0:T(8,128)S(1)} %copy-done, f32[128,2,8]{0,2,1:T(8,128)S(1)} %select_maximum_fusion.2, pred[128,512]{0,1:T(8,128)(4,1)S(1)} %compare_and_fusion.2, f32[128,2,8,128]{0,3,2,1:T(8,128)S(1)} %get-tuple-element.426, f32[128,2,8]{0,2,1:T(8,128)S(1)} %get-tuple-element.409, ...), kind=kOutput, calls=%fused_computation.11.clone.1 | convolution fusion | flops 273416192 | bytes 6635525 | tf_op jit(solution)/shard_map/cond/branch_1_fun/while/body/eval_jaxpr/rkgt,tkd->rkgd/dot_general | solution.py:59
  69.0 0.7 dynamic_slice.40
  69.6 0.7 iota_add_fusion.3
  70.3 0.1 convert_reduce_fusion.3
  70.4 0.2 compare_and_fusion.2
  70.6 2.6 %fusion.39 = (f32[128,2,8]{0,2,1:T(8,128)S(1)}, f32[2,512,128,8]{2,1,3,0:T(8,128)}) fusion(pred[128,512]{0,1:T(8,128)(4,1)S(1)} %compare_and_fusion.2, bf16[128,2,8,128]{3,0,2,1:T(8,128)(2,1)S(1)} %get-tuple-element.445, bf16[2,512,2,128]{3,1,0,2:T(8,128)(2,1)S(1)} %get-tuple-element.444, s32[]{:T(128)} %get-tuple-element.423), kind=kOutput, calls=%fused_computation.4.clone.1 | convolution fusion | flops 271579136 | bytes 5054468 | tf_op jit(solution)/shard_map/cond/branch_1_fun/while/body/eval_jaxpr/rkgd,tkd->rkgt/dot_general | solution.py:50
  73.3 0.0 copy-start
  73.3 3.2 %fusion.40 = f32[128,2,8]{0,2,1:T(8,128)S(1)} fusion(f32[2,512,128,8]{2,1,3,0:T(8,128)} %get-tuple-element.407, f32[128,2,8]{0,2,1:T(8,128)S(1)} %select_maximum_fusion.2, pred[128,512]{0,1:T(8,128)(4,1)S(1)} %compare_and_fusion.2), kind=kLoop, calls=%fused_computation.3.clone.1 | loop fusion | flops 4192256 | bytes 4276224 | tf_op jit(solution)/shard_map/cond/branch_1_fun/while/body/eval_jaxpr/reduce_sum | solution.py:58
  76.5 1.3 %fusion.41 = (f32[128,2,8]{0,2,1:T(8,128)}, f32[128,2,8]{0,2,1:T(8,128)S(1)}) fusion(f32[128,2,8]{0,2,1:T(8,128)S(1)} %fusion.40, f32[128,2,8]{0,2,1:T(8,128)} %get-tuple-element.425, pred[]{:T(512)S(6)} %compare.27, f32[128,2,8]{0,2,1:T(8,128)S(1)} %select_maximum_fusion.2, f32[128,2,8]{0,2,1:T(8,128)S(1)} %get-tuple-element.424), kind=kLoop, calls=%fused_computation.20.clone.1 | loop fusion | flops 10240 | bytes 49153 | tf_op jit(solution)/shard_map/cond/branch_1_fun/while/body/eval_jaxpr/add | solution.py:58
  77.8 0.0 copy-done
  77.8 1.3 %fusion.42 = f32[128,2,8,128]{0,3,2,1:T(8,128)S(1)} fusion(f32[2,512,128,8]{2,1,3,0:T(8,128)S(1)} %copy-done, f32[128,2,8]{0,2,1:T(8,128)S(1)} %select_maximum_fusion.2, pred[128,512]{0,1:T(8,128)(4,1)S(1)} %compare_and_fusion.2, f32[128,2,8,128]{0,3,2,1:T(8,128)S(1)} %get-tuple-element.426, f32[128,2,8]{0,2,1:T(8,128)S(1)} %get-tuple-element.409, ...), kind=kOutput, calls=%fused_computation.11.clone.1 | convolution fusion | flops 273416192 | bytes 6635525 | tf_op jit(solution)/shard_map/cond/branch_1_fun/while/body/eval_jaxpr/rkgt,tkd->rkgd/dot_general | solution.py:59
  79.2 0.5 copy.38
  79.7 0.8 %copy.32 = f32[128,2,8]{2,1,0:T(2,128)S(1)} copy(f32[128,2,8]{0,2,1:T(8,128)} %get-tuple-element.197) | data formatting | bytes 16384 | tf_op jit(solution)/shard_map/cond | solution.py:75
  80.5 1.1 %divide_convert_fusion = bf16[128,2,8,128]{3,2,1,0:T(8,128)(2,1)} fusion(f32[128,2,8,128]{3,2,1,0:T(8,128)S(1)} %get-tuple-element.300, f32[128,2,8]{2,1,0:T(2,128)S(1)} %copy.32), kind=kLoop, calls=%fused_computation.31 | loop fusion | flops 524288 | bytes 1581056 | tf_op jit(solution)/shard_map/convert_element_type | solution.py:78
  (18 shorter events, 0.2 us)
Async XLA Ops:
  0.9 40.5 %collective-permute-start = (bf16[128,2,128]{2,0,1:T(8,128)(2,1)S(1)}, bf16[128,2,128]{2,0,1:T(8,128)(2,1)S(1)}, u32[]{:S(2)}, u32[]{:S(2)}) collective-permute-start(bf16[128,2,128]{2,0,1:T(8,128)(2,1)S(1)} %get-tuple-element.329), channel_id=1, source_target_pairs={{0,14},{2,0},{4,2},{6,4},{8,6},{10,8},{12,10},{14,12},{1,15},{3,1}... | collective-permute-start | bytes 196616 | tf_op jit(solution)/shard_map/ppermute | solution.py:16
  41.4 5.5 %collective-permute-start.1 = (bf16[256,2,128]{2,0,1:T(8,128)(2,1)S(1)}, bf16[256,2,128]{2,0,1:T(8,128)(2,1)S(1)}, u32[]{:S(2)}, u32[]{:S(2)}) collective-permute-start(bf16[256,2,128]{2,0,1:T(8,128)(2,1)S(1)} %pad_maximum_fusion.1), channel_id=1, source_target_pairs={{0,12},{2,14},{4,0},{6,2},{8,4},{10,6},{12,8},{14,10},{1,13},{3,15... | collective-permute-start | bytes 393224 | tf_op jit(solution)/shard_map/ppermute | solution.py:16
  46.9 10.1 %collective-permute-start.2 = (bf16[512,2,128]{2,0,1:T(8,128)(2,1)S(1)}, bf16[512,2,128]{2,0,1:T(8,128)(2,1)S(1)}, u32[]{:S(2)}, u32[]{:S(2)}) collective-permute-start(bf16[512,2,128]{2,0,1:T(8,128)(2,1)S(1)} %pad_maximum_fusion), channel_id=1, source_target_pairs={{0,8},{2,10},{4,12},{6,14},{8,0},{10,2},{12,4},{14,6},{1,9},{3,11}... | collective-permute-start | bytes 786440 | tf_op jit(solution)/shard_map/ppermute | solution.py:16
  63.8 3.8 %copy-start = (f32[2,512,128,8]{2,1,3,0:T(8,128)S(1)}, f32[2,512,128,8]{2,1,3,0:T(8,128)}, u32[]{:S(2)}) copy-start(f32[2,512,128,8]{2,1,3,0:T(8,128)} %get-tuple-element.407) | copy-start | bytes 12582916 | tf_op jit(solution)/shard_map/cond/branch_1_fun/while
  73.3 4.5 %copy-start = (f32[2,512,128,8]{2,1,3,0:T(8,128)S(1)}, f32[2,512,128,8]{2,1,3,0:T(8,128)}, u32[]{:S(2)}) copy-start(f32[2,512,128,8]{2,1,3,0:T(8,128)} %get-tuple-element.407) | copy-start | bytes 12582916 | tf_op jit(solution)/shard_map/cond/branch_1_fun/while
